TPU v7x, 256 devices: a whole 4x4x8 slice. The times are simulated.
256 devices in a mesh: inp: 4 (over y_hi, core), dep: 8 (over x, y_lo), out: 8 (over z).
Axes of the slice: x: 4, y: 4 (y_hi: 2, y_lo: 2; y = y_hi * 2 + y_lo), z: 8, core: 2. Of those that a mesh axis runs over, the one named last changes fastest.
Arguments:
- tokens: bfloat16 [1024, 16384], P('inp', 'out'), may hold values from -6 to 6
- gate_up_weight: bfloat16 [16384, 2, 28672], P('out', None, ('inp', 'dep')), may hold values from -0.046875 to 0.046875
- down_weight: bfloat16 [28672, 16384], P(('inp', 'dep'), 'out'), may hold values from -0.03125 to 0.03125
Outputs:
- layer_output: bfloat16 [1024, 16384], P(('inp', 'dep'), 'out')
All inputs are finite; a program needn't handle non-finite values.
Results may differ from a plain program's by a relative error of at most 0.0049.
Values may be sent and summed in bfloat16 or wider, within the bound.
A program may use at most 128 MiB of HBM per device.

v0:
```python
import jax
import jax.numpy as jnp
from jax import lax
from jax.sharding import PartitionSpec as P


def swiglu(projected):
    return (jax.nn.silu(projected[:, 0, :]) * projected[:, 1, :]).astype(jnp.bfloat16)


def shards(tokens, gate_up_weight, down_weight):
    local_width = gate_up_weight.shape[0]
    block_units = gate_up_weight.shape[2]
    flat_weight = gate_up_weight.reshape(local_width, 2 * block_units)
    projected = jnp.dot(
        lax.all_gather(tokens, "inp", axis=0, tiled=True),
        flat_weight,
        preferred_element_type=jnp.float32,
    )
    projected = projected.reshape(projected.shape[0], 2, block_units)
    totals = lax.psum(projected, "out")
    full_hidden = swiglu(totals)
    result = lax.psum_scatter(
        jnp.dot(full_hidden, down_weight, preferred_element_type=jnp.float32),
        ("inp", "dep"),
        scatter_dimension=0,
        tiled=True,
    )
    return result.astype(jnp.bfloat16)


def solution(mesh):
    placed = (P("inp", "out"), P("out", None, ("inp", "dep")), P(("inp", "dep"), "out"))
    return jax.shard_map(
        shards, mesh=mesh, in_specs=placed, out_specs=P(("inp", "dep"), "out"), check_vma=False
    )
```

profile of v0, /device:TPU:10, one launch (start us, length us, event | category | flops | bytes accessed | tf_op | source)
XLA Modules:
  0.0 443.8 jit_solution(10383628695858579418)
XLA Ops:
  6.5 0.0 all-gather.2.cloned.1.call-start
  6.5 0.7 all-gather.2.cloned.1.call-update
  7.3 0.0 all-reduce.2.cloned.1.call-start
  7.3 7.6 %copy.5 = bf16[256,8,2,896]{3,1,2,0:T(8,128)(2,1)} copy(bf16[256,8,2,896]{3,2,1,0:T(2,128)(2,1)} %bitcast.23) | data formatting | bytes 14680064
  14.9 10.5 %copy.4 = bf16[1792,2048]{1,0:T(8,128)(2,1)} copy(bf16[1792,2048]{0,1:T(8,128)(2,1)} %bitcast.22) | data formatting | bytes 14680064 | tf_op jit(solution)/shard_map/dot_general | solution.py:15
  25.4 26.8 %all-gather.2.cloned.1.call-done = bf16[1024,2048]{1,0:T(8,128)(2,1)} async-done(((bf16[256,2048]{1,0:T(8,128)(2,1)}), bf16[1024,2048]{1,0:T(8,128)(2,1)}) %all-gather.2.cloned.1.call-update) | async-done | bytes 4194320 | tf_op jit(solution)/shard_map/all_gather | solution.py:16
  52.3 14.3 %fusion = f32[1024,2,896]{2,0,1:T(8,128)} fusion(bf16[2,896,2048]{2,1,0:T(8,128)(2,1)} %bitcast.24, bf16[1024,2048]{1,0:T(8,128)(2,1)} %all-gather.2.cloned.1.call-done), kind=kOutput, calls=%fused_computation | convolution fusion | flops 7516192768 | bytes 18874368 | tf_op jit(solution)/shard_map/dot_general | solution.py:15
  66.5 0.0 all-reduce.2.cloned.1.call-update
  66.6 0.0 reduce-scatter.2.cloned.1.call-start
  66.6 168.7 %all-reduce.2.cloned.1.call-done = f32[1024,2,896]{2,0,1:T(8,128)} async-done(((f32[1024,2,896]{2,0,1:T(8,128)}), f32[1024,2,896]{2,0,1:T(8,128)}) %all-reduce.2.cloned.1.call-update) | async-done | bytes 7340048 | tf_op jit(solution)/shard_map/psum | solution.py:21
  235.3 11.9 %fusion.4 = f32[1024,2048]{1,0:T(8,128)} fusion(bf16[896,2048]{1,0:T(8,128)(2,1)} %param.5, f32[1024,2,896]{2,0,1:T(8,128)} %all-reduce.2.cloned.1.call-done), kind=kOutput, calls=%fused_computation.6 | convolution fusion | flops 3763601408 | bytes 19398656 | tf_op jit(solution)/shard_map/dot_general | solution.py:24
  247.3 0.0 reduce-scatter.2.cloned.1.call-update
  247.3 188.3 %reduce-scatter.2.cloned.1.call-done = f32[32,2048]{1,0:T(8,128)} async-done(((f32[1024,2048]{1,0:T(8,128)}), f32[32,2048]{1,0:T(8,128)}) %reduce-scatter.2.cloned.1.call-update) | async-done | bytes 262160 | tf_op jit(solution)/shard_map/reduce_scatter | solution.py:23
  435.6 1.6 convert_element_type.7
Async XLA Ops:
  6.5 45.7 %all-gather.2.cloned.1.call-start = ((), (), s32[]{:S(2)}) async-start(), calls=%async_computation.1 | async-start | bytes 5242880 | tf_op jit(solution)/shard_map/all_gather | solution.py:16
  7.3 228.1 %all-reduce.2.cloned.1.call-start = ((), (), s32[]{:S(2)}) async-start(), calls=%async_computation.2 | async-start | bytes 14680064 | tf_op jit(solution)/shard_map/psum | solution.py:21
  66.6 369.1 %reduce-scatter.2.cloned.1.call-start = ((), (), s32[]{:S(2)}) async-start(), calls=%async_computation.3 | async-start | bytes 8650752 | tf_op jit(solution)/shard_map/reduce_scatter | solution.py:23
Sparse Core Ops, SparseCore 0:
  9.2 43.0 all-gather.1
  66.7 168.5 all-reduce.1
  247.4 188.1 reduce-scatter.1
where the time goes:
time: 444 us
  waiting for transfers between devices  385 us (87%)
  matrix products  26.2 us (6%)
  local copies, waits for them, and re-layouts  18.1 us (4%)
  between operations  13.1 us (3%)
    reduce_scatter x1, waiting for transfers between devices, shards(): lax.psum_scatter(jnp.dot(full_hidden, down_weight, preferred_element_type...  188 us
    psum x1, waiting for transfers between devices, shards(): totals = lax.psum(projected, 'out')  169 us
    all_gather x1, waiting for transfers between devices, shards(): lax.all_gather(tokens, 'inp', axis=0, tiled=True)  26.8 us
    dot_general x1, matrix products, shards(): jnp.dot(lax.all_gather(tokens, 'inp', axis=0, tiled=True), flat_weight, p...  14.3 us
    dot_general x1, matrix products, shards(): jnp.dot(full_hidden, down_weight, preferred_element_type=jnp.float32)  11.9 us
    dot_general x1, local copies, waits for them, and re-layouts, shards(): jnp.dot(lax.all_gather(tokens, 'inp', axis=0, tiled=True), flat_weight, p...  10.5 us
  transfers between devices with their start and end apart: 3, of which 3 were waited for; matrix products, arithmetic and copies ran while one was open for 4% of the time, Pallas kernels for 0%

commit v1 on v0

--- a/solution.py
+++ b/solution.py
@@ -18,7 +18,7 @@
         preferred_element_type=jnp.float32,
     )
     projected = projected.reshape(projected.shape[0], 2, block_units)
-    totals = lax.psum(projected, "out")
+    totals = jnp.sum(lax.all_gather(projected, "out"), axis=0)
     full_hidden = swiglu(totals)
     result = lax.psum_scatter(
         jnp.dot(full_hidden, down_weight, preferred_element_type=jnp.float32),

time: 444 us -> 864 us (1.95)
  waiting for transfers between devices: 385 us -> 782 us
  other arithmetic: 1.62 us -> 23.5 us
    all_gather x0 -> x1, waiting for transfers between devices: none -> 566 us  [shards(): totals = jnp.sum(lax.all_gather(projected, 'out'), axis=0)]
    psum x1 -> x0, waiting for transfers between devices: 169 us -> none  [shards(): totals = lax.psum(projected, 'out')]
    reduce_sum x0 -> x1, other arithmetic: none -> 21.9 us  [shards(): totals = jnp.sum(lax.all_gather(projected, 'out'), axis=0)]
  transfers between devices with their start and end apart: 3 -> 3, of which waited for: 3 -> 3; matrix products, arithmetic and copies ran while one was open for 4% -> 2% of each run, Pallas kernels for 0% -> 0%
where the time goes in v1:
time: 864 us; the launch traced here: 863 us
  waiting for transfers between devices  782 us (91%)
  matrix products  26.1 us (3%)
  other arithmetic  23.5 us (3%)
  local copies, waits for them, and re-layouts  18.1 us (2%)
  between operations  13.1 us (2%)
    all_gather x1, waiting for transfers between devices, shards(): totals = jnp.sum(lax.all_gather(projected, 'out'), axis=0)  566 us
    reduce_scatter x1, waiting for transfers between devices, shards(): lax.psum_scatter(jnp.dot(full_hidden, down_weight, preferred_element_type...  188 us
    all_gather x1, waiting for transfers between devices, shards(): lax.all_gather(tokens, 'inp', axis=0, tiled=True)  26.8 us
    reduce_sum x1, other arithmetic, shards(): totals = jnp.sum(lax.all_gather(projected, 'out'), axis=0)  21.9 us
  transfers between devices with their start and end apart: 3, of which 3 were waited for; matrix products, arithmetic and copies ran while one was open for 2% of the time, Pallas kernels for 0%

profile of v1, /device:TPU:10, one launch (start us, length us, event | category | flops | bytes accessed | tf_op | source)
XLA Modules:
  0.0 863.1 jit_solution(13905271145227306760)
XLA Ops:
  6.5 0.0 all-gather.4.cloned.1.call-start
  6.5 0.7 all-gather.4.cloned.1.call-update
  7.3 0.0 all-gather.6.cloned.1.call-start
  7.3 7.6 copy.7
  14.9 10.5 %copy.6 = bf16[1792,2048]{1,0:T(8,128)(2,1)} copy(bf16[1792,2048]{0,1:T(8,128)(2,1)} %bitcast.24) | data formatting | bytes 14680064 | tf_op jit(solution)/shard_map/dot_general | solution.py:15
  25.4 26.8 %all-gather.4.cloned.1.call-done = bf16[1024,2048]{1,0:T(8,128)(2,1)} async-done(((bf16[256,2048]{1,0:T(8,128)(2,1)}), bf16[1024,2048]{1,0:T(8,128)(2,1)}) %all-gather.4.cloned.1.call-update) | async-done | bytes 4194320 | tf_op jit(solution)/shard_map/all_gather | solution.py:16
  52.3 14.2 %fusion = f32[1024,2,896]{2,0,1:T(8,128)} fusion(bf16[2,896,2048]{2,1,0:T(8,128)(2,1)} %bitcast.26, bf16[1024,2048]{1,0:T(8,128)(2,1)} %all-gather.4.cloned.1.call-done), kind=kOutput, calls=%fused_computation | convolution fusion | flops 7516192768 | bytes 18874368 | tf_op jit(solution)/shard_map/dot_general | solution.py:15
  66.4 0.0 all-gather.6.cloned.1.call-update
  66.5 0.0 reduce-scatter.2.cloned.1.call-start
  66.5 566.4 %all-gather.6.cloned.1.call-done = f32[8192,2,896]{2,0,1:T(8,128)} async-done(((f32[1024,2,896]{2,0,1:T(8,128)}), f32[8192,2,896]{2,0,1:T(8,128)}) %all-gather.6.cloned.1.call-update) | async-done | bytes 58720272 | tf_op jit(solution)/shard_map/all_gather | solution.py:21
  632.9 21.9 %reduce_sum.9 = f32[1024,2,896]{2,0,1:T(8,128)} reduce(f32[8,1024,2,896]{3,1,0,2:T(8,128)} %bitcast.23, f32[]{:T(128)} %constant.1.clone.1), dimensions={0}, to_apply=%region_0.0 | reduce | flops 12845056 | bytes 66060292 | tf_op jit(solution)/shard_map/reduce_sum | solution.py:21
  654.9 11.9 %fusion.4 = f32[1024,2048]{1,0:T(8,128)} fusion(bf16[896,2048]{1,0:T(8,128)(2,1)} %param.5, f32[1024,2,896]{2,0,1:T(8,128)} %reduce_sum.9), kind=kOutput, calls=%fused_computation.6 | convolution fusion | flops 3763601408 | bytes 19398656 | tf_op jit(solution)/shard_map/dot_general | solution.py:24
  666.8 0.0 reduce-scatter.2.cloned.1.call-update
  666.8 188.1 %reduce-scatter.2.cloned.1.call-done = f32[32,2048]{1,0:T(8,128)} async-done(((f32[1024,2048]{1,0:T(8,128)}), f32[32,2048]{1,0:T(8,128)}) %reduce-scatter.2.cloned.1.call-update) | async-done | bytes 262160 | tf_op jit(solution)/shard_map/reduce_scatter | solution.py:23
  854.9 1.6 convert_element_type.7
Async XLA Ops:
  6.5 45.7 %all-gather.4.cloned.1.call-start = ((), (), s32[]{:S(2)}) async-start(), calls=%async_computation.1 | async-start | bytes 5242880 | tf_op jit(solution)/shard_map/all_gather | solution.py:16
  7.3 625.7 %all-gather.6.cloned.1.call-start = ((), (), s32[]{:S(2)}) async-start(), calls=%async_computation.3 | async-start | bytes 66060288 | tf_op jit(solution)/shard_map/all_gather | solution.py:21
  66.5 788.5 %reduce-scatter.2.cloned.1.call-start = ((), (), s32[]{:S(2)}) async-start(), calls=%async_computation.2 | async-start | bytes 8650752 | tf_op jit(solution)/shard_map/reduce_scatter | solution.py:23
Sparse Core Ops, SparseCore 0:
  9.2 43.0 all-gather.3
  66.6 566.2 all-gather.5
  667.0 187.9 reduce-scatter.1
